TPU v7x, 32 devices: a whole 2x2x4 slice. The times are simulated.
32 devices in a mesh: seq: 8 (over y, x, core), exp: 4 (over z).
Axes of the slice: x: 2, y: 2, z: 4, core: 2. Of those that a mesh axis runs over, the one named last changes fastest.
Arguments:
- queries: bfloat16 [1024, 2048], P('seq', 'exp'), may hold values from -10 to 10
- key_rows: bfloat16 [1024, 2048], P('seq', 'exp'), may hold values from -10 to 10
- value_rows: bfloat16 [1024, 2048], P('seq', 'exp'), may hold values from -6 to 6
- residual: bfloat16 [1024, 2048], P('seq'), may hold values from -20 to 20
- out_weight: bfloat16 [2048, 2048], P('exp'), may hold values from -1 to 1
- norm_gain: float32 [2048], replicated, may hold values from 0.5 to 1.5
- gate_weight: bfloat16 [16, 2048, 1408], P('seq', None, 'exp'), may hold values from -0.125 to 0.125
- up_weight: bfloat16 [16, 2048, 1408], P('seq', None, 'exp'), may hold values from -0.125 to 0.125
- down_weight: bfloat16 [16, 1408, 2048], P('seq', 'exp'), may hold values from -0.15625 to 0.15625
- routes: int32 [1024, 6], P('seq'), may hold values from 0 to 15, all different within a row; in each aligned block of 128 rows (0 to 127, 128 to 255, ...) at most 96 rows name the same one
- route_gates: float32 [1024, 6], P('seq'), may hold values from 0.2 to 1
- block_picks: int32 [2, 3], replicated, may hold values from 0 to 1, as said below
Outputs:
- layer_out: bfloat16 [1024, 2048], P(('seq', 'exp'))
Inputs may be any that keep to these rules, and one draw needn't show every extreme that they name: `block_picks`: row b names block b first, then blocks at or before b, repeats allowed. `routes`: in each aligned block of 128 rows no expert is named by more than 96 rows, a bound that some block reaches.
All inputs are finite; a program needn't handle non-finite values.
Results may differ from a plain program's by a relative error of at most 0.015.
Values may be sent and summed in bfloat16 or wider, within the bound.
No kernel may reach another device: no remote copies, remote signals or barrier semaphores. Data moves between devices by JAX's collectives and lax.ppermute only.
A program may use at most 64 MiB of HBM per device.

v0:
```python
import jax
import jax.numpy as jnp
from jax import lax
from jax.sharding import PartitionSpec as P

HD = 128
TOPK = 6
BLK = 512


def rms_scale(hidden, norm_gain):
    mean_square = jnp.mean(hidden * hidden, axis=-1, keepdims=True)
    return hidden * lax.rsqrt(mean_square + 1e-06) * norm_gain


def expert_block(arrived, gate_weight, up_weight, down_weight):
    gate_part = jnp.einsum(
        "semd,edf->semf", arrived, gate_weight, preferred_element_type=jnp.float32
    )
    up_part = jnp.einsum("semd,edf->semf", arrived, up_weight, preferred_element_type=jnp.float32)
    inner_act = (jax.nn.silu(gate_part) * up_part).astype(jnp.bfloat16)
    return jnp.einsum(
        "semf,efd->semd", inner_act, down_weight, preferred_element_type=jnp.float32
    ).astype(jnp.bfloat16)


def per_device(
    queries,
    key_rows,
    value_rows,
    residual,
    out_weight,
    norm_gain,
    gate_weight,
    up_weight,
    down_weight,
    routes,
    route_gates,
    block_picks,
):
    seq_count = lax.axis_size("seq")
    exp_count = lax.axis_size("exp")
    seq_index = lax.axis_index("seq")
    exp_index = lax.axis_index("exp")
    tok_rows = queries.shape[0]
    head_count = queries.shape[1] // HD
    nblocks = block_picks.shape[0]
    model_width = residual.shape[1]
    positions = seq_index * tok_rows + jnp.arange(tok_rows, dtype=jnp.int32)
    block_ids = jnp.arange(nblocks, dtype=jnp.int32)
    chosen = jnp.any(block_picks[:, :, None] == block_ids[None, None, :], axis=1).astype(
        jnp.float32
    )
    query_onehot = ((positions // BLK)[:, None] == block_ids[None, :]).astype(jnp.float32)
    query_allowed = jnp.dot(query_onehot, chosen)
    split_queries = queries.reshape(tok_rows, head_count, HD)
    score_scale = HD ** (-0.5)
    run_max = jnp.full((tok_rows, head_count), -1e30, jnp.float32)
    key_piece = lax.all_gather(key_rows, "seq", axis=0, tiled=True)
    value_piece = lax.all_gather(value_rows, "seq", axis=0, tiled=True)
    piece_rows = key_piece.shape[0]
    key_pos = jnp.arange(piece_rows, dtype=jnp.int32)
    key_onehot = ((key_pos // BLK)[:, None] == block_ids[None, :]).astype(jnp.float32)
    allowed = (
        (jnp.dot(query_allowed, key_onehot.T) > 0.5) & (key_pos[None, :] <= positions[:, None])
    )[:, None, :]
    scores = (
        jnp.einsum(
            "qhd,khd->qhk",
            split_queries,
            key_piece.reshape(piece_rows, head_count, HD),
            preferred_element_type=jnp.float32,
        )
        * score_scale
    )
    piece_max = jnp.max(jnp.where(allowed, scores, -1e30), axis=2)
    new_max = jnp.maximum(run_max, piece_max)
    expo = jnp.where(allowed, jnp.exp(scores - new_max[:, :, None]), 0.0)
    new_total = jnp.sum(expo, axis=2)
    mixed_values = jnp.einsum(
        "qhk,khd->qhd",
        expo.astype(jnp.bfloat16),
        value_piece.reshape(piece_rows, head_count, HD),
        preferred_element_type=jnp.float32,
    )
    attended = (
        (mixed_values / new_total[:, :, None])
        .astype(jnp.bfloat16)
        .reshape(tok_rows, head_count * HD)
    )
    proj_part = jnp.dot(attended, out_weight, preferred_element_type=jnp.float32)
    share_rows = tok_rows // exp_count
    projected = lax.psum_scatter(
        proj_part.astype(jnp.bfloat16), "exp", scatter_dimension=0, tiled=True
    ).astype(jnp.float32)
    own_residual = lax.dynamic_slice_in_dim(residual, exp_index * share_rows, share_rows, 0).astype(
        jnp.float32
    )
    own_hidden = own_residual + projected
    own_normed = rms_scale(own_hidden, norm_gain).astype(jnp.bfloat16)
    normed = lax.all_gather(own_normed, "exp", axis=0, tiled=True)
    local_experts = gate_weight.shape[0]
    expert_count = local_experts * seq_count
    slot_most = exp_count * max(1, 2 * tok_rows * TOPK // (expert_count * exp_count))
    slot_total = expert_count * slot_most
    pair_count = tok_rows * TOPK
    flat_routes = routes.reshape(pair_count)
    route_onehot = (
        flat_routes[:, None] == jnp.arange(expert_count, dtype=jnp.int32)[None, :]
    ).astype(jnp.int32)
    slot_rank = jnp.sum((jnp.cumsum(route_onehot, axis=0) - 1) * route_onehot, axis=1)
    slot_ids = flat_routes * slot_most + slot_rank
    sources = (
        jnp.full((slot_total,), pair_count, jnp.int32)
        .at[slot_ids]
        .set(jnp.arange(pair_count, dtype=jnp.int32))
    )
    live_slot = sources < pair_count
    token_ids = jnp.minimum(sources, pair_count - 1) // TOPK
    outgoing = jnp.where(live_slot[:, None], normed[token_ids], jnp.zeros((), jnp.bfloat16))
    outgoing = outgoing.reshape(seq_count, local_experts, slot_most, model_width)
    returned = lax.all_to_all(
        expert_block(
            lax.all_to_all(outgoing, "seq", split_axis=0, concat_axis=0, tiled=True),
            gate_weight,
            up_weight,
            down_weight,
        ),
        "seq",
        split_axis=0,
        concat_axis=0,
        tiled=True,
    )
    back_rows = returned.reshape(slot_total, model_width)[slot_ids].astype(jnp.float32)
    weighted = back_rows.reshape(tok_rows, TOPK, model_width) * route_gates[:, :, None]
    mixture_part = jnp.sum(weighted, axis=1)
    own_mixture = lax.psum_scatter(
        mixture_part.astype(jnp.bfloat16), "exp", scatter_dimension=0, tiled=True
    ).astype(jnp.float32)
    return (own_hidden + own_mixture).astype(jnp.bfloat16)


def solution(mesh):
    placed = (
        P("seq", "exp"),
        P("seq", "exp"),
        P("seq", "exp"),
        P("seq", None),
        P("exp", None),
        P(),
        P("seq", None, "exp"),
        P("seq", None, "exp"),
        P("seq", "exp", None),
        P("seq", None),
        P("seq", None),
        P(),
    )
    return jax.shard_map(
        per_device, mesh=mesh, in_specs=placed, out_specs=P(("seq", "exp"), None), check_vma=False
    )
```

profile of v0, /device:TPU:0, one launch (start us, length us, event | category | flops | bytes accessed | tf_op | source)
XLA Modules:
  0.0 345.7 jit_solution(12460206369254408509)
XLA Ops:
  6.5 1.8 copy.47
  11.8 1.7 reduce-window.6
  13.5 22.0 %all-gather.3.cloned.1.call-done = bf16[1024,512]{0,1:T(8,128)(2,1)} async-done(((bf16[128,512]{0,1:T(8,128)(2,1)}), bf16[1024,512]{0,1:T(8,128)(2,1)}) %all-gather.3.cloned.1.call-update) | async-done | bytes 1048592 | tf_op jit(solution)/shard_map/all_gather | solution.py:59
  35.4 1.9 fusion.11
  39.1 21.6 %all-gather.5.cloned.1.call-done = bf16[1024,512]{1,0:T(8,128)(2,1)} async-done(((bf16[128,512]{1,0:T(8,128)(2,1)}), bf16[1024,512]{1,0:T(8,128)(2,1)}) %all-gather.5.cloned.1.call-update) | async-done | bytes 1048592 | tf_op jit(solution)/shard_map/all_gather | solution.py:60
  60.7 2.3 copy.50
  63.0 2.7 fusion.26
  67.9 3.4 scatter_custom_fusion
  71.4 17.6 %reduce-scatter.3.cloned.1.call-done = bf16[32,2048]{1,0:T(8,128)(2,1)} async-done(((bf16[128,2048]{1,0:T(8,128)(2,1)}), bf16[32,2048]{1,0:T(8,128)(2,1)}) %reduce-scatter.3.cloned.1.call-update) | async-done | bytes 131088 | tf_op jit(solution)/shard_map/reduce_scatter | solution.py:93
  91.3 15.4 %all_gather.11 = bf16[128,2048]{1,0:T(8,128)(2,1)S(1)} all-gather(bf16[32,2048]{1,0:T(8,128)(2,1)S(1)} %multiply_convert_fusion), channel_id=1, replica_groups=mesh['seq'=8,'exp'=4] {'exp'}, dimensions={0}, use_global_device_ids=true | all-gather | bytes 655360 | tf_op jit(solution)/shard_map/all_gather | solution.py:101
  106.6 7.1 %gather_fusion = bf16[1536,2048]{1,0:T(8,128)(2,1)} fusion(bf16[128,2048]{1,0:T(8,128)(2,1)S(1)} %all_gather.11, s32[2048]{0:T(1024)S(1)} %pad_clamp_fusion), kind=kCustom, calls=%fused_computation | custom fusion | bytes 12589056 | tf_op jit(solution)/shard_map/gather | solution.py:120
  113.7 3.3 broadcast_select_fusion
  117.0 75.3 %all_to_all.10 = bf16[8,2,96,2048]{3,2,1,0:T(8,128)(2,1)S(1)} all-to-all(bf16[8,2,96,2048]{3,2,1,0:T(8,128)(2,1)S(1)} %broadcast_select_fusion), channel_id=1, replica_groups=mesh['seq'=8,'exp'=4] {'seq'}, dimensions={0} | all-to-all | bytes 12582912 | tf_op jit(solution)/shard_map/all_to_all | solution.py:124
  192.4 2.7 copy-done.3
  195.0 4.8 %fusion.2 = f32[2,8,96,352]{3,2,1,0:T(8,128)} fusion(bf16[8,2,96,2048]{3,2,1,0:T(8,128)(2,1)S(1)} %all_to_all.10, bf16[2,2048,352]{1,2,0:T(8,128)(2,1)S(1)} %copy-done.9), kind=kOutput, calls=%fused_computation.8 | convolution fusion | flops 2214592512 | bytes 11337728 | tf_op jit(solution)/shard_map/semd,edf->semf/dot_general | solution.py:17
  199.9 11.2 %convert_bitcast_fusion = bf16[8,2,96,2048]{3,2,0,1:T(8,128)(2,1)} fusion(bf16[2,352,2048]{2,1,0:T(8,128)(2,1)S(1)} %copy-done, f32[2,8,96,352]{3,2,1,0:T(8,128)} %fusion.2, bf16[2,2048,352]{1,2,0:T(8,128)(2,1)} %param.19, bf16[8,2,96,2048]{3,2,1,0:T(8,128)(2,1)} %copy-done.3), kind=kOutput, calls=%fused_computation.4 | convolution fusion | flops 4435574784 | bytes 20512768 | tf_op jit(solution)/shard_map/semf,efd->semd/dot_general | solution.py:22
  211.1 6.6 %copy.58 = bf16[8,2,96,2048]{3,2,1,0:T(8,128)(2,1)} copy(bf16[8,2,96,2048]{3,2,0,1:T(8,128)(2,1)} %convert_bitcast_fusion) | data formatting | bytes 12582912 | tf_op jit(solution)/shard_map/convert_element_type | solution.py:24
  217.7 4.9 %all-to-all-start.1 = ((bf16[8,2,96,2048]{3,2,1,0:T(8,128)(2,1)}), bf16[8,2,96,2048]{3,2,1,0:T(8,128)(2,1)}, u32[]{:S(2)}, u32[]{:S(2)}) async-start(bf16[8,2,96,2048]{3,2,1,0:T(8,128)(2,1)} %copy.58), calls=%async_computation.2 | async-start | bytes 12582912 | tf_op jit(solution)/shard_map/all_to_all | solution.py:122
  223.0 71.2 %all-to-all-done.1 = bf16[8,2,96,2048]{3,2,1,0:T(8,128)(2,1)} async-done(((bf16[8,2,96,2048]{3,2,1,0:T(8,128)(2,1)}), bf16[8,2,96,2048]{3,2,1,0:T(8,128)(2,1)}, u32[]{:S(2)}, u32[]{:S(2)}) %all-to-all-start.1) | async-done | bytes 6291488 | tf_op jit(solution)/shard_map/all_to_all | solution.py:122
  294.1 10.7 %gather_fusion.1 = bf16[768,2048]{1,0:T(8,128)(2,1)} fusion(bf16[1536,2048]{1,0:T(8,128)(2,1)} %bitcast.16, s32[1024]{0:T(1024)S(1)} %pad_clamp_fusion.1), kind=kCustom, calls=%fused_computation.1 | custom fusion | bytes 6294528 | tf_op jit(solution)/shard_map/gather | solution.py:134
  304.8 6.7 %reshape.131 = f32[128,6,2048]{2,1,0:T(8,128)} reshape(bf16[768,2048]{1,0:T(8,128)(2,1)} %gather_fusion.1) | data formatting | bytes 9437184 | tf_op jit(solution)/shard_map/convert_element_type | solution.py:134
  311.5 7.4 %multiply_reduce_fusion = bf16[128,2048]{1,0:T(8,128)(2,1)} fusion(f32[128,6,2048]{2,1,0:T(8,128)} %reshape.131, f32[128,6]{1,0:T(8,128)S(1)} %copy.59), kind=kLoop, calls=%fused_computation.3 | loop fusion | flops 2883584 | bytes 6818816 | tf_op jit(solution)/shard_map/reduce_sum | solution.py:136
  319.0 18.5 %reduce-scatter.5.cloned.1.call-done = bf16[32,2048]{1,0:T(8,128)(2,1)} async-done(((bf16[128,2048]{1,0:T(8,128)(2,1)}), bf16[32,2048]{1,0:T(8,128)(2,1)}) %reduce-scatter.5.cloned.1.call-update) | async-done | bytes 131088 | tf_op jit(solution)/shard_map/reduce_scatter | solution.py:137
  337.5 1.7 add_convert_fusion
  (56 shorter events, 9.9 us)
Async XLA Ops:
  6.5 193.3 %copy-start = (bf16[2,352,2048]{2,1,0:T(8,128)(2,1)S(1)}, bf16[2,352,2048]{2,1,0:T(8,128)(2,1)}, u32[]{:S(2)}) copy-start(bf16[2,352,2048]{2,1,0:T(8,128)(2,1)} %param.20) | copy-start | bytes 8650756
  6.5 28.9 %all-gather.3.cloned.1.call-start = ((), (), s32[]{:S(2)}) async-start(), calls=%async_computation.4 | async-start | bytes 1179648 | tf_op jit(solution)/shard_map/all_gather | solution.py:59
  8.4 52.4 %all-gather.5.cloned.1.call-start = ((), (), s32[]{:S(2)}) async-start(), calls=%async_computation.5 | async-start | bytes 1179648 | tf_op jit(solution)/shard_map/all_gather | solution.py:60
  9.1 79.9 %reduce-scatter.3.cloned.1.call-start = ((), (), s32[]{:S(2)}) async-start(), calls=%async_computation.6 | async-start | bytes 655360 | tf_op jit(solution)/shard_map/reduce_scatter | solution.py:93
  37.3 1.4 copy-start.2
  63.0 2.8 copy-start.4
  65.8 1.7 copy-start.6
  65.8 24.4 %copy-start.7 = (f32[2048]{0:T(1024)S(1)}, f32[2048]{0:T(1024)}, u32[]{:S(2)}) copy-start(f32[2048]{0:T(1024)} %param.17) | copy-start | bytes 24580
  117.0 78.0 %copy-start.9 = (bf16[2,2048,352]{1,2,0:T(8,128)(2,1)S(1)}, bf16[2,2048,352]{1,2,0:T(8,128)(2,1)}, u32[]{:S(2)}) copy-start(bf16[2,2048,352]{1,2,0:T(8,128)(2,1)} %param.18) | copy-start | bytes 8650756
  192.4 2.7 copy-start.3
  217.7 5.2 %copy-start.8 = (f32[128,6]{0,1:T(8,128)S(1)}, f32[128,6]{0,1:T(8,128)}, u32[]{:S(2)}) copy-start(f32[128,6]{0,1:T(8,128)} %param.22) | copy-start | bytes 9220
  217.7 76.4 %all-to-all-start.1 = ((bf16[8,2,96,2048]{3,2,1,0:T(8,128)(2,1)}), bf16[8,2,96,2048]{3,2,1,0:T(8,128)(2,1)}, u32[]{:S(2)}, u32[]{:S(2)}) async-start(bf16[8,2,96,2048]{3,2,1,0:T(8,128)(2,1)} %copy.58), calls=%async_computation.2 | async-start | bytes 12582912 | tf_op jit(solution)/shard_map/all_to_all | solution.py:122
  222.6 115.0 %reduce-scatter.5.cloned.1.call-start = ((), (), s32[]{:S(2)}) async-start(), calls=%async_computation.7 | async-start | bytes 655360 | tf_op jit(solution)/shard_map/reduce_scatter | solution.py:137
  304.8 34.4 %copy-start.1 = (bf16[2,352,2048]{2,1,0:T(8,128)(2,1)S(1)}, bf16[2,352,2048]{2,1,0:T(8,128)(2,1)}, u32[]{:S(2)}) copy-start(bf16[2,352,2048]{2,1,0:T(8,128)(2,1)} %param.20) | copy-start | bytes 8650756
  311.5 26.0 %copy-start.5 = (bf16[32,2048]{1,0:T(8,128)(2,1)S(1)}, bf16[32,2048]{1,0:T(8,128)(2,1)}, u32[]{:S(2)}) copy-start(bf16[32,2048]{1,0:T(8,128)(2,1)} %reduce-scatter.3.cloned.1.call-done) | copy-start | bytes 393220
Sparse Core Ops, SparseCore 0:
  9.2 26.1 all-gather.2
  37.3 23.3 all-gather.4
  67.2 21.8 reduce-scatter.2
  319.1 18.3 reduce-scatter.4
where the time goes:
time: 346 us
  waiting for transfers between devices  152 us (44%)
  blocking collectives  90.7 us (26%)
  local copies, waits for them, and re-layouts  44.6 us (13%)
  matrix products  22.5 us (7%)
  other arithmetic  17.8 us (5%)
  between operations  13.3 us (4%)
  starting transfers between devices  5.21 us (2%)
    all_to_all x1, blocking collectives, per_device(): lax.all_to_all(outgoing, 'seq', split_axis=0, concat_axis=0, tiled=True)  75.3 us
    all_to_all x1, waiting for transfers between devices, per_device(): lax.all_to_all(expert_block(lax.all_to_all(outgoing, 'seq', split_axis=0,...  71.2 us
    all_gather x1, waiting for transfers between devices, per_device(): key_piece = lax.all_gather(key_rows, 'seq', axis=0, tiled=True)  22 us
    all_gather x1, waiting for transfers between devices, per_device(): value_piece = lax.all_gather(value_rows, 'seq', axis=0, tiled=True)  21.6 us
    reduce_scatter x1, waiting for transfers between devices, per_device(): lax.psum_scatter(mixture_part.astype(jnp.bfloat16), 'exp', scatter_dimens...  18.5 us
    reduce_scatter x1, waiting for transfers between devices, per_device(): lax.psum_scatter(proj_part.astype(jnp.bfloat16), 'exp', scatter_dimension...  17.6 us
    all_gather x1, blocking collectives, per_device(): normed = lax.all_gather(own_normed, 'exp', axis=0, tiled=True)  15.4 us
    dot_general x1, matrix products, expert_block(): jnp.einsum('semf,efd->semd', inner_act, down_weight, preferred_element_ty...  11.2 us
  transfers between devices with their start and end apart: 5, of which 5 were waited for; matrix products, arithmetic and copies ran while one was open for 3% of the time, Pallas kernels for 0%

commit v1 on v0

--- a/solution.py
+++ b/solution.py
@@ -6,6 +6,28 @@
 HD = 128
 TOPK = 6
 BLK = 512
+
+
+def in_order(tiles, dim):
+    tiles = jnp.moveaxis(tiles, 0, dim)
+    lengths = tiles.shape
+    return tiles.reshape(*lengths[:dim], lengths[dim] * lengths[dim + 1], *lengths[dim + 2 :])
+
+
+def ring_gather(array, axis, dim):
+    size = lax.axis_size(axis)
+    pairs = [(i, (i + 1) % size) for i in range(size)]
+    back = [(b, a) for a, b in pairs]
+    lower, upper = ([], [])
+    for hop in range(size - 1):
+        if hop % 2 == 0:
+            lower.append(lax.ppermute(lower[-1] if lower else array, axis, pairs))
+        else:
+            upper.append(lax.ppermute(upper[-1] if upper else array, axis, back))
+    pieces = jnp.stack([*lower[::-1], array, *upper])
+    shift = lax.axis_index(axis) - len(lower)
+    pieces = pieces[(jnp.arange(size) - shift) % size]
+    return in_order(pieces, dim)
 
 
 def rms_scale(hidden, norm_gain):
@@ -56,7 +78,7 @@
     split_queries = queries.reshape(tok_rows, head_count, HD)
     score_scale = HD ** (-0.5)
     run_max = jnp.full((tok_rows, head_count), -1e30, jnp.float32)
-    key_piece = lax.all_gather(key_rows, "seq", axis=0, tiled=True)
+    key_piece = ring_gather(key_rows, "seq", 0)
     value_piece = lax.all_gather(value_rows, "seq", axis=0, tiled=True)
     piece_rows = key_piece.shape[0]
     key_pos = jnp.arange(piece_rows, dtype=jnp.int32)

time: 346 us -> 336 us (0.971)
  waiting for transfers between devices: 152 us -> 118 us
  local copies, waits for them, and re-layouts: 44.6 us -> 58.5 us
  starting transfers between devices: 5.21 us -> 14 us
    all_gather x1 -> x0, waiting for transfers between devices: 22 us -> none  [per_device(): key_piece = lax.all_gather(key_rows, 'seq', axis=0, tiled=True)]
    all_gather x1, waiting for transfers between devices: 21.6 us -> 0.02 us  [per_device(): value_piece = lax.all_gather(value_rows, 'seq', axis=0, tiled=True)]
    ppermute x0 -> x7, waiting for transfers between devices: none -> 10.3 us  [the longest x4 10.3 us: ring_gather(): lower.append(lax.ppermute(lower[-1] if lower else array, axis, pairs))]
    ppermute x0 -> x7, starting transfers between devices: none -> 8.81 us  [the longest x3 8.31 us: ring_gather(): upper.append(lax.ppermute(upper[-1] if upper else array, axis, back))]
    unnamed x23 -> x33, local copies, waits for them, and re-layouts: 6.75 us -> 14.1 us
  transfers between devices with their start and end apart: 5 -> 11, of which waited for: 5 -> 6; matrix products, arithmetic and copies ran while one was open for 3% -> 8% of each run, Pallas kernels for 0% -> 0%
where the time goes in v1:
time: 336 us
  waiting for transfers between devices  118 us (35%)
  blocking collectives  90.7 us (27%)
  local copies, waits for them, and re-layouts  58.5 us (17%)
  matrix products  23 us (7%)
  other arithmetic  17.8 us (5%)
  starting transfers between devices  14 us (4%)
  between operations  13.4 us (4%)
    all_to_all x1, blocking collectives, per_device(): lax.all_to_all(outgoing, 'seq', split_axis=0, concat_axis=0, tiled=True)  75.2 us
    all_to_all x1, waiting for transfers between devices, per_device(): lax.all_to_all(expert_block(lax.all_to_all(outgoing, 'seq', split_axis=0,...  71.2 us
    reduce_scatter x1, waiting for transfers between devices, per_device(): lax.psum_scatter(mixture_part.astype(jnp.bfloat16), 'exp', scatter_dimens...  18.5 us
    reduce_scatter x1, waiting for transfers between devices, per_device(): lax.psum_scatter(proj_part.astype(jnp.bfloat16), 'exp', scatter_dimension...  18.2 us
    all_gather x1, blocking collectives, per_device(): normed = lax.all_gather(own_normed, 'exp', axis=0, tiled=True)  15.4 us
    unnamed x33, local copies, waits for them, and re-layouts  14.1 us
    dot_general x1, matrix products, expert_block(): jnp.einsum('semf,efd->semd', inner_act, down_weight, preferred_element_ty...  11.2 us
    gather x1, local copies, waits for them, and re-layouts, per_device(): returned.reshape(slot_total, model_width)[slot_ids].astype(jnp.float32)  10.7 us
  transfers between devices with their start and end apart: 11, of which 6 were waited for; matrix products, arithmetic and copies ran while one was open for 8% of the time, Pallas kernels for 0%

profile of v1, /device:TPU:0, one launch (start us, length us, event | category | flops | bytes accessed | tf_op | source)
XLA Modules:
  0.0 335.6 jit_solution(16027864273944082968)
XLA Ops:
  7.0 2.9 collective-permute-start.4
  14.0 4.2 %collective-permute-done.1 = bf16[128,512]{1,0:T(8,128)(2,1)} collective-permute-done((bf16[128,512]{1,0:T(8,128)(2,1)S(1)}, bf16[128,512]{1,0:T(8,128)(2,1)}, u32[]{:S(2)}, u32[]{:S(2)}) %collective-permute-start.1) | collective-permute-done | bytes 131104 | tf_op jit(solution)/shard_map/ppermute | solution.py:24
  18.2 2.7 collective-permute-start.5
  20.9 5.1 %collective-permute-done.2 = bf16[128,512]{1,0:T(8,128)(2,1)} collective-permute-done((bf16[128,512]{1,0:T(8,128)(2,1)}, bf16[128,512]{1,0:T(8,128)(2,1)}, u32[]{:S(2)}, u32[]{:S(2)}) %collective-permute-start.2) | collective-permute-done | bytes 131104 | tf_op jit(solution)/shard_map/ppermute | solution.py:24
  28.9 2.7 collective-permute-start.6
  41.4 2.9 gather_fusion
  50.1 2.3 copy.48
  52.4 2.7 fusion.26
  57.2 3.4 %scatter_custom_fusion = s32[1536]{0:T(1024)S(1)} fusion(s32[768]{0:T(1024)S(1)} %fusion.52, s32[768]{0:T(1024)S(1)} %iota.41, s32[]{:T(128)} %constant.99.clone.1), kind=kCustom, calls=%fused_computation.85 | custom fusion | bytes 6148 | tf_op jit(solution)/shard_map/scatter | solution.py:138
  60.8 18.2 %reduce-scatter.3.cloned.1.call-done = bf16[32,2048]{1,0:T(8,128)(2,1)} async-done(((bf16[128,2048]{1,0:T(8,128)(2,1)}), bf16[32,2048]{1,0:T(8,128)(2,1)}) %reduce-scatter.3.cloned.1.call-update) | async-done | bytes 131088 | tf_op jit(solution)/shard_map/reduce_scatter | solution.py:115
  81.2 15.4 %all_gather.7 = bf16[128,2048]{1,0:T(8,128)(2,1)S(1)} all-gather(bf16[32,2048]{1,0:T(8,128)(2,1)S(1)} %multiply_convert_fusion), channel_id=1, replica_groups=mesh['seq'=8,'exp'=4] {'exp'}, dimensions={0}, use_global_device_ids=true | all-gather | bytes 655360 | tf_op jit(solution)/shard_map/all_gather | solution.py:123
  96.6 7.1 %gather_fusion.1 = bf16[1536,2048]{1,0:T(8,128)(2,1)} fusion(bf16[128,2048]{1,0:T(8,128)(2,1)S(1)} %all_gather.7, s32[2048]{0:T(1024)S(1)} %pad_clamp_fusion), kind=kCustom, calls=%fused_computation.1 | custom fusion | bytes 12589056 | tf_op jit(solution)/shard_map/gather | solution.py:142
  103.7 3.3 broadcast_select_fusion
  107.0 75.2 %all_to_all.10 = bf16[8,2,96,2048]{3,2,1,0:T(8,128)(2,1)S(1)} all-to-all(bf16[8,2,96,2048]{3,2,1,0:T(8,128)(2,1)S(1)} %broadcast_select_fusion), channel_id=1, replica_groups=mesh['seq'=8,'exp'=4] {'seq'}, dimensions={0} | all-to-all | bytes 12582912 | tf_op jit(solution)/shard_map/all_to_all | solution.py:146
  182.2 2.7 copy-done.2
  184.9 4.8 %fusion.2 = f32[2,8,96,352]{3,2,1,0:T(8,128)} fusion(bf16[8,2,96,2048]{3,2,1,0:T(8,128)(2,1)S(1)} %all_to_all.10, bf16[2,2048,352]{1,2,0:T(8,128)(2,1)S(1)} %copy-done.11), kind=kOutput, calls=%fused_computation.9 | convolution fusion | flops 2214592512 | bytes 11337728 | tf_op jit(solution)/shard_map/semd,edf->semf/dot_general | solution.py:39
  189.8 11.2 %convert_bitcast_fusion = bf16[8,2,96,2048]{3,2,0,1:T(8,128)(2,1)} fusion(bf16[2,352,2048]{2,1,0:T(8,128)(2,1)S(1)} %copy-done, f32[2,8,96,352]{3,2,1,0:T(8,128)} %fusion.2, bf16[2,2048,352]{1,2,0:T(8,128)(2,1)} %param.19, bf16[8,2,96,2048]{3,2,1,0:T(8,128)(2,1)} %copy-done.2), kind=kOutput, calls=%fused_computation.5 | convolution fusion | flops 4435574784 | bytes 20512768 | tf_op jit(solution)/shard_map/semf,efd->semd/dot_general | solution.py:44
  201.0 6.6 %copy.56 = bf16[8,2,96,2048]{3,2,1,0:T(8,128)(2,1)} copy(bf16[8,2,96,2048]{3,2,0,1:T(8,128)(2,1)} %convert_bitcast_fusion) | data formatting | bytes 12582912 | tf_op jit(solution)/shard_map/convert_element_type | solution.py:46
  207.6 4.9 %all-to-all-start.1 = ((bf16[8,2,96,2048]{3,2,1,0:T(8,128)(2,1)}), bf16[8,2,96,2048]{3,2,1,0:T(8,128)(2,1)}, u32[]{:S(2)}, u32[]{:S(2)}) async-start(bf16[8,2,96,2048]{3,2,1,0:T(8,128)(2,1)} %copy.56), calls=%async_computation.2 | async-start | bytes 12582912 | tf_op jit(solution)/shard_map/all_to_all | solution.py:144
  212.8 71.2 %all-to-all-done.1 = bf16[8,2,96,2048]{3,2,1,0:T(8,128)(2,1)} async-done(((bf16[8,2,96,2048]{3,2,1,0:T(8,128)(2,1)}), bf16[8,2,96,2048]{3,2,1,0:T(8,128)(2,1)}, u32[]{:S(2)}, u32[]{:S(2)}) %all-to-all-start.1) | async-done | bytes 6291488 | tf_op jit(solution)/shard_map/all_to_all | solution.py:144
  284.0 10.7 %gather_fusion.2 = bf16[768,2048]{1,0:T(8,128)(2,1)} fusion(bf16[1536,2048]{1,0:T(8,128)(2,1)} %bitcast.24, s32[1024]{0:T(1024)S(1)} %pad_clamp_fusion.1), kind=kCustom, calls=%fused_computation.2 | custom fusion | bytes 6294528 | tf_op jit(solution)/shard_map/gather | solution.py:156
  294.7 6.7 %reshape.176 = f32[128,6,2048]{2,1,0:T(8,128)} reshape(bf16[768,2048]{1,0:T(8,128)(2,1)} %gather_fusion.2) | data formatting | bytes 9437184 | tf_op jit(solution)/shard_map/convert_element_type | solution.py:156
  301.4 7.4 %multiply_reduce_fusion = bf16[128,2048]{1,0:T(8,128)(2,1)} fusion(f32[128,6,2048]{2,1,0:T(8,128)} %reshape.176, f32[128,6]{1,0:T(8,128)S(1)} %copy.57), kind=kLoop, calls=%fused_computation.4 | loop fusion | flops 2883584 | bytes 6818816 | tf_op jit(solution)/shard_map/reduce_sum | solution.py:158
  308.9 18.5 %reduce-scatter.5.cloned.1.call-done = bf16[32,2048]{1,0:T(8,128)(2,1)} async-done(((bf16[128,2048]{1,0:T(8,128)(2,1)}), bf16[32,2048]{1,0:T(8,128)(2,1)}) %reduce-scatter.5.cloned.1.call-update) | async-done | bytes 131088 | tf_op jit(solution)/shard_map/reduce_scatter | solution.py:159
  (82 shorter events, 29.4 us)
Async XLA Ops:
  6.5 183.2 %copy-start = (bf16[2,352,2048]{2,1,0:T(8,128)(2,1)S(1)}, bf16[2,352,2048]{2,1,0:T(8,128)(2,1)}, u32[]{:S(2)}) copy-start(bf16[2,352,2048]{2,1,0:T(8,128)(2,1)} %param.20) | copy-start | bytes 8650756
  6.5 31.4 %copy-start.6 = (bf16[128,512]{1,0:T(8,128)(2,1)S(1)}, bf16[128,512]{1,0:T(8,128)(2,1)}, u32[]{:S(2)}) copy-start(bf16[128,512]{1,0:T(8,128)(2,1)} %param.13) | copy-start | bytes 393220
  6.5 43.5 %all-gather.2.cloned.1.call-start = ((), (), s32[]{:S(2)}) async-start(), calls=%async_computation.4 | async-start | bytes 1179648 | tf_op jit(solution)/shard_map/all_gather | solution.py:82
  6.5 6.3 %collective-permute-start = (bf16[128,512]{1,0:T(8,128)(2,1)}, bf16[128,512]{1,0:T(8,128)(2,1)S(1)}, u32[]{:S(2)}, u32[]{:S(2)}) collective-permute-start(bf16[128,512]{1,0:T(8,128)(2,1)} %param.13), channel_id=1, source_target_pairs={{0,4},{4,8},{8,12},{12,16},{16,20},{20,24},{24,28},{28,0},{1,5},{5... | collective-permute-start | bytes 393224 | tf_op jit(solution)/shard_map/ppermute | solution.py:24
  7.0 11.2 %collective-permute-start.4 = (bf16[128,512]{1,0:T(8,128)(2,1)}, bf16[128,512]{1,0:T(8,128)(2,1)S(1)}, u32[]{:S(2)}, u32[]{:S(2)}) collective-permute-start(bf16[128,512]{1,0:T(8,128)(2,1)} %param.13), channel_id=1, source_target_pairs={{4,0},{8,4},{12,8},{16,12},{20,16},{24,20},{28,24},{0,28},{5,1},{9... | collective-permute-start | bytes 393224 | tf_op jit(solution)/shard_map/ppermute | solution.py:26
  10.0 69.0 %reduce-scatter.3.cloned.1.call-start = ((), (), s32[]{:S(2)}) async-start(), calls=%async_computation.5 | async-start | bytes 655360 | tf_op jit(solution)/shard_map/reduce_scatter | solution.py:115
  12.8 13.2 %copy-start.7 = (bf16[128,512]{1,0:T(8,128)(2,1)}, bf16[128,512]{1,0:T(8,128)(2,1)S(1)}, u32[]{:S(2)}) copy-start(bf16[128,512]{1,0:T(8,128)(2,1)S(1)} %collective-permute-done) | copy-start | bytes 393220
  12.8 5.4 %collective-permute-start.1 = (bf16[128,512]{1,0:T(8,128)(2,1)S(1)}, bf16[128,512]{1,0:T(8,128)(2,1)}, u32[]{:S(2)}, u32[]{:S(2)}) collective-permute-start(bf16[128,512]{1,0:T(8,128)(2,1)S(1)} %collective-permute-done), channel_id=1, source_target_pairs={{0,4},{4,8},{8,12},{12,16},{16,20},{20,24},{24,28},{28,0},{1,5},{5... | collective-permute-start | bytes 393224 | tf_op jit(solution)/shard_map/ppermute | solution.py:24
  18.2 7.8 %collective-permute-start.2 = (bf16[128,512]{1,0:T(8,128)(2,1)}, bf16[128,512]{1,0:T(8,128)(2,1)}, u32[]{:S(2)}, u32[]{:S(2)}) collective-permute-start(bf16[128,512]{1,0:T(8,128)(2,1)} %collective-permute-done.1), channel_id=1, source_target_pairs={{0,4},{4,8},{8,12},{12,16},{16,20},{20,24},{24,28},{28,0},{1,5},{5... | collective-permute-start | bytes 393224 | tf_op jit(solution)/shard_map/ppermute | solution.py:24
  18.2 10.7 %collective-permute-start.5 = (bf16[128,512]{1,0:T(8,128)(2,1)S(1)}, bf16[128,512]{1,0:T(8,128)(2,1)}, u32[]{:S(2)}, u32[]{:S(2)}) collective-permute-start(bf16[128,512]{1,0:T(8,128)(2,1)S(1)} %collective-permute-done.4), channel_id=1, source_target_pairs={{4,0},{8,4},{12,8},{16,12},{20,16},{24,20},{28,24},{0,28},{5,1},{9... | collective-permute-start | bytes 393224 | tf_op jit(solution)/shard_map/ppermute | solution.py:26
  26.0 5.6 %collective-permute-start.3 = (bf16[128,512]{1,0:T(8,128)(2,1)}, bf16[128,512]{1,0:T(8,128)(2,1)}, u32[]{:S(2)}, u32[]{:S(2)}) collective-permute-start(bf16[128,512]{1,0:T(8,128)(2,1)} %collective-permute-done.2), channel_id=1, source_target_pairs={{0,4},{4,8},{8,12},{12,16},{16,20},{20,24},{24,28},{28,0},{1,5},{5... | collective-permute-start | bytes 393224 | tf_op jit(solution)/shard_map/ppermute | solution.py:24
  28.9 11.8 %collective-permute-start.6 = (bf16[128,512]{1,0:T(8,128)(2,1)}, bf16[128,512]{1,0:T(8,128)(2,1)S(1)}, u32[]{:S(2)}, u32[]{:S(2)}) collective-permute-start(bf16[128,512]{1,0:T(8,128)(2,1)} %collective-permute-done.5), channel_id=1, source_target_pairs={{4,0},{8,4},{12,8},{16,12},{20,16},{24,20},{28,24},{0,28},{5,1},{9... | collective-permute-start | bytes 393224 | tf_op jit(solution)/shard_map/ppermute | solution.py:26
  48.2 1.4 copy-start.4
  52.4 2.8 copy-start.3
  55.1 1.7 copy-start.8
  55.1 25.0 %copy-start.9 = (f32[2048]{0:T(1024)S(1)}, f32[2048]{0:T(1024)}, u32[]{:S(2)}) copy-start(f32[2048]{0:T(1024)} %param.17) | copy-start | bytes 24580
  107.0 77.9 %copy-start.11 = (bf16[2,2048,352]{1,2,0:T(8,128)(2,1)S(1)}, bf16[2,2048,352]{1,2,0:T(8,128)(2,1)}, u32[]{:S(2)}) copy-start(bf16[2,2048,352]{1,2,0:T(8,128)(2,1)} %param.18) | copy-start | bytes 8650756
  182.2 2.7 copy-start.2
  207.6 5.2 %copy-start.10 = (f32[128,6]{0,1:T(8,128)S(1)}, f32[128,6]{0,1:T(8,128)}, u32[]{:S(2)}) copy-start(f32[128,6]{0,1:T(8,128)} %param.22) | copy-start | bytes 9220
  207.6 76.4 %all-to-all-start.1 = ((bf16[8,2,96,2048]{3,2,1,0:T(8,128)(2,1)}), bf16[8,2,96,2048]{3,2,1,0:T(8,128)(2,1)}, u32[]{:S(2)}, u32[]{:S(2)}) async-start(bf16[8,2,96,2048]{3,2,1,0:T(8,128)(2,1)} %copy.56), calls=%async_computation.2 | async-start | bytes 12582912 | tf_op jit(solution)/shard_map/all_to_all | solution.py:144
  212.4 115.0 %reduce-scatter.5.cloned.1.call-start = ((), (), s32[]{:S(2)}) async-start(), calls=%async_computation.6 | async-start | bytes 655360 | tf_op jit(solution)/shard_map/reduce_scatter | solution.py:159
  294.7 34.4 %copy-start.1 = (bf16[2,352,2048]{2,1,0:T(8,128)(2,1)S(1)}, bf16[2,352,2048]{2,1,0:T(8,128)(2,1)}, u32[]{:S(2)}) copy-start(bf16[2,352,2048]{2,1,0:T(8,128)(2,1)} %param.20) | copy-start | bytes 8650756
  301.4 26.0 %copy-start.5 = (bf16[32,2048]{1,0:T(8,128)(2,1)S(1)}, bf16[32,2048]{1,0:T(8,128)(2,1)}, u32[]{:S(2)}) copy-start(bf16[32,2048]{1,0:T(8,128)(2,1)} %reduce-scatter.3.cloned.1.call-done) | copy-start | bytes 393220
Sparse Core Ops, SparseCore 0:
  10.1 27.6 all-gather.1
  56.5 22.3 reduce-scatter.2
  309.0 18.3 reduce-scatter.4
